TPU v7x, 32 devices: a whole 2x2x4 slice. The times are simulated.
32 devices in a mesh: sc: 4 (over y, x), rows: 8 (over z, core).
Axes of the slice: x: 2, y: 2, z: 4, core: 2. Of those that a mesh axis runs over, the one named last changes fastest.
Arguments:
- embeddings: bfloat16 [32768, 1024], P(('sc', 'rows')), may hold values from -6 to 6
- labels: int32 [32768, 1], P(('sc', 'rows')), may hold values from 0 to 3; in each aligned block of 1024 rows (0 to 1023, 1024 to 2047, ...) at most 512 rows name the same one
- init_idx: int32 [4, 256], P('sc'), may hold values from 0 to 16383
Outputs:
- assign: bfloat16 [32768, 256], P(('sc', 'rows'))
- centroids: float32 [4, 256, 1024], P('sc')
Inputs may be any that keep to these rules, and one draw needn't show every extreme that they name: `labels`: among the rows of one device (aligned blocks of 1024 rows) no label occurs more than 512 times, and some label occurs exactly 512 times; every label occurs somewhere.
All inputs are finite; a program needn't handle non-finite values.
Results may differ from a plain program's by a relative error of at most 0.0052.
Values may be sent and summed in bfloat16 or wider, within the bound.
A program may use at most 64 MiB of HBM per device.

v0:
```python
import math

import jax
import jax.numpy as jnp
from jax import lax
from jax.sharding import PartitionSpec as P

ITERS = 3
ROUNDS = 3


def carried_in(part, axis, combine, identity):
    place = lax.axis_index(axis)
    gathered = lax.all_gather(part, axis)
    state = jnp.zeros_like(part) + jnp.asarray(identity, part.dtype)

    def one(turn, state):
        return combine(state, lax.dynamic_index_in_dim(gathered, turn, 0, False))

    return lax.fori_loop(0, place, one, state)


def unit_of(rows):
    values = rows.astype(jnp.float32)
    scale = lax.rsqrt(jnp.mean(values * values, axis=1, keepdims=True) + 1e-05) * (
        1.0 / math.sqrt(rows.shape[1])
    )
    return (values * scale).astype(jnp.bfloat16)


def unit_cent(mass):
    return (mass * lax.rsqrt(jnp.sum(mass * mass, axis=1, keepdims=True) + 1e-06)).astype(
        jnp.bfloat16
    )


def on_device(embeddings, labels, init_idx):
    tok = embeddings.shape[0]
    width = embeddings.shape[1]
    groups = lax.axis_size("sc")
    slots = 2 * tok // groups
    label_col = labels[:, 0]
    member = (label_col[:, None] == jnp.arange(groups, dtype=jnp.int32)[None, :]).astype(jnp.int32)
    before_here = jnp.cumsum(member, axis=0) - member
    place = jnp.sum(before_here * member, axis=1)
    counts = jnp.sum(member, axis=0).astype(jnp.float32)
    prefix = carried_in(
        counts, ("sc", "rows"), lambda early, later: early + later, jnp.zeros_like(counts)
    )
    totals = lax.psum(counts, ("sc", "rows"))
    prefix_int = prefix.astype(jnp.int32)
    totals_int = totals.astype(jnp.int32)
    rank = jnp.sum(member * prefix_int[None, :], axis=1) + place
    target = label_col * slots + place
    source = (
        jnp.full((groups * slots,), tok, jnp.int32).at[target].set(jnp.arange(tok, dtype=jnp.int32))
    )
    padded = jnp.concatenate([embeddings, jnp.zeros((1, width), jnp.bfloat16)], axis=0)
    rank_pad = jnp.concatenate([rank, jnp.full((1,), -1, jnp.int32)], axis=0)
    outgoing = padded[source].reshape(groups, slots, width)
    out_rank = rank_pad[source].reshape(groups, slots)
    incoming, in_rank = (
        lax.all_to_all(outgoing, "sc", split_axis=0, concat_axis=0, tiled=True),
        lax.all_to_all(out_rank, "sc", split_axis=0, concat_axis=0, tiled=True),
    )
    incoming = incoming.reshape(groups * slots, width)
    in_rank = in_rank.reshape(groups * slots)
    valid = in_rank >= 0
    members = unit_of(incoming)
    group_here = lax.axis_index("sc")
    count = jnp.sum(jnp.where(jnp.arange(groups, dtype=jnp.int32) == group_here, totals_int, 0))
    wanted = init_idx[0] % count
    picker = (wanted[:, None] == in_rank[None, :]).astype(jnp.bfloat16)
    seeds = jnp.dot(picker, members, preferred_element_type=jnp.float32)
    cent = lax.psum(seeds, "rows").astype(jnp.bfloat16)
    contract_rows = (((0,), (0,)), ((), ()))
    contract_width = (((1,), (1,)), ((), ()))
    for round_index in range(ROUNDS):
        scores = lax.dot_general(members, cent, contract_width, preferred_element_type=jnp.float32)
        plan = jnp.where(valid[:, None], jnp.exp(scores * 10.0), 0.0)
        for step in range(ITERS):
            column = lax.psum(jnp.sum(plan, axis=0), "rows")
            plan = plan / column[None, :]
            row_sum = jnp.sum(plan, axis=1)
            plan = jnp.where(valid[:, None], plan / jnp.where(valid, row_sum, 1.0)[:, None], 0.0)
        plan_b = plan.astype(jnp.bfloat16)
        mass_part = lax.dot_general(
            plan_b, members, contract_rows, preferred_element_type=jnp.float32
        )
        if round_index < ROUNDS - 1:
            mass = lax.psum(mass_part, "rows")
            cent = unit_cent(mass)
        else:
            weight_part = jnp.sum(plan, axis=0)
            mass, weight = lax.psum((mass_part, weight_part), "rows")
            means = mass / weight[:, None]
    plan_out = plan.astype(jnp.bfloat16).reshape(groups, slots, plan.shape[1])
    returned = lax.all_to_all(plan_out, "sc", split_axis=0, concat_axis=0, tiled=True).reshape(
        groups * slots, plan.shape[1]
    )
    assign = returned[target]
    return (assign, means[None])


def solution(mesh):
    return jax.shard_map(
        on_device,
        mesh=mesh,
        in_specs=(P(("sc", "rows"), None), P(("sc", "rows"), None), P("sc", None)),
        out_specs=(P(("sc", "rows"), None), P("sc", None, None)),
        check_vma=False,
    )
```

profile of v0, /device:TPU:0, one launch (start us, length us, event | category | flops | bytes accessed | tf_op | source)
XLA Modules:
  0.0 568.7 jit_solution(1118507430221130394)
XLA Ops:
  8.1 42.0 %all-reduce.2 = (f32[128]{0:T(128)S(1)}, f32[4]{0:T(128)S(1)}) all-reduce(f32[128]{0:T(128)S(1)} %convert_dynamic-update-slice_fusion, f32[4]{0:T(128)S(1)} %convert_element_type.59), channel_id=2, replica_groups=mesh['sc'=4,'rows'=8] {'sc','rows'}, use_global_device_ids=true, to_apply=%add.1 | all-reduce | flops 132 | bytes 1056
  54.0 4.3 scatter_custom_fusion
  58.4 20.6 %gather_fusion = s32[2048]{0:T(1024)} fusion(s32[1025]{0:T(1024)S(1)} %pad_add_fusion, s32[2048]{0:T(1024)S(1)} %fusion.27), kind=kCustom, calls=%fused_computation | custom fusion | bytes 24576 | tf_op jit(solution)/shard_map/gather | solution.py:61
  78.9 4.4 all-to-all-start
  85.1 9.7 %gather_fusion.1 = bf16[2048,1024]{1,0:T(8,128)(2,1)} fusion(bf16[1025,1024]{1,0:T(8,128)(2,1)S(1)} %concatenate.7, s32[2048]{0:T(1024)S(1)} %fusion.27), kind=kCustom, calls=%fused_computation.1 | custom fusion | bytes 8396800 | tf_op jit(solution)/shard_map/gather | solution.py:60
  94.8 5.0 all-to-all-start.1
  101.9 44.5 %all-to-all-done.1 = bf16[4,512,1024]{2,1,0:T(8,128)(2,1)} async-done(((bf16[4,512,1024]{2,1,0:T(8,128)(2,1)}), bf16[4,512,1024]{2,1,0:T(8,128)(2,1)}, u32[]{:S(2)}, u32[]{:S(2)}) %all-to-all-start.1) | async-done | bytes 4194336 | tf_op jit(solution)/shard_map/all_to_all | solution.py:63
  146.5 3.1 multiply_reduce_fusion
  149.6 2.9 fusion
  155.8 57.9 %all-reduce.13 = bf16[256,1024]{1,0:T(8,128)(2,1)S(1)} all-reduce(f32[256,1024]{1,0:T(8,128)S(1)} %fusion.7), channel_id=1, replica_groups=mesh['sc'=4,'rows'=8] {'rows'}, use_global_device_ids=true, to_apply=%region_11.12 | all-reduce | flops 262144 | bytes 1572864 | tf_op jit(solution)/shard_map/psum | solution.py:75
  213.7 3.2 fusion.41
  216.8 15.1 %psum.107 = f32[256]{0:T(256)S(1)} all-reduce(f32[256]{0:T(256)S(1)} %get-tuple-element.52), channel_id=1, replica_groups=mesh['sc'=4,'rows'=8] {'rows'}, use_global_device_ids=true, to_apply=%region_13.14 | all-reduce | flops 256 | bytes 2048 | tf_op jit(solution)/shard_map/psum | solution.py:82
  234.3 13.6 %psum.108 = f32[256]{0:T(256)S(1)} all-reduce(f32[256]{0:T(256)S(1)} %get-tuple-element.48), channel_id=1, replica_groups=mesh['sc'=4,'rows'=8] {'rows'}, use_global_device_ids=true, to_apply=%region_16.17 | all-reduce | flops 256 | bytes 2048 | tf_op jit(solution)/shard_map/psum | solution.py:82
  250.0 13.7 %psum.109 = f32[256]{0:T(256)S(1)} all-reduce(f32[256]{0:T(256)S(1)} %get-tuple-element.46), channel_id=1, replica_groups=mesh['sc'=4,'rows'=8] {'rows'}, use_global_device_ids=true, to_apply=%region_19.20 | all-reduce | flops 256 | bytes 2048 | tf_op jit(solution)/shard_map/psum | solution.py:82
  265.7 4.9 fusion.9
  270.9 56.0 %all-reduce.8.cloned.1.call-done = f32[256,1024]{1,0:T(8,128)} async-done(((f32[256,1024]{1,0:T(8,128)}), f32[256,1024]{1,0:T(8,128)}) %all-reduce.8.cloned.1.call-update) | async-done | bytes 1048592 | tf_op jit(solution)/shard_map/psum | solution.py:91
  328.2 3.6 fusion.42
  331.8 13.6 %psum.111 = f32[256]{0:T(256)S(1)} all-reduce(f32[256]{0:T(256)S(1)} %get-tuple-element.54), channel_id=1, replica_groups=mesh['sc'=4,'rows'=8] {'rows'}, use_global_device_ids=true, to_apply=%region_24.25 | all-reduce | flops 256 | bytes 2048 | tf_op jit(solution)/shard_map/psum | solution.py:82
  347.7 13.6 %psum.112 = f32[256]{0:T(256)S(1)} all-reduce(f32[256]{0:T(256)S(1)} %get-tuple-element.44), channel_id=1, replica_groups=mesh['sc'=4,'rows'=8] {'rows'}, use_global_device_ids=true, to_apply=%region_27.28 | all-reduce | flops 256 | bytes 2048 | tf_op jit(solution)/shard_map/psum | solution.py:82
  363.4 13.7 %psum.113 = f32[256]{0:T(256)S(1)} all-reduce(f32[256]{0:T(256)S(1)} %get-tuple-element.42), channel_id=1, replica_groups=mesh['sc'=4,'rows'=8] {'rows'}, use_global_device_ids=true, to_apply=%region_30.31 | all-reduce | flops 256 | bytes 2048 | tf_op jit(solution)/shard_map/psum | solution.py:82
  379.1 4.9 fusion.10
  384.1 57.0 %all-reduce.10.cloned.1.call-done = f32[256,1024]{1,0:T(8,128)} async-done(((f32[256,1024]{1,0:T(8,128)}), f32[256,1024]{1,0:T(8,128)}) %all-reduce.10.cloned.1.call-update) | async-done | bytes 1048592 | tf_op jit(solution)/shard_map/psum | solution.py:91
  442.5 3.6 fusion.43
  446.1 13.6 %psum.115 = f32[256]{0:T(256)S(1)} all-reduce(f32[256]{0:T(256)S(1)} %get-tuple-element.56), channel_id=1, replica_groups=mesh['sc'=4,'rows'=8] {'rows'}, use_global_device_ids=true, to_apply=%region_35.36 | all-reduce | flops 256 | bytes 2048 | tf_op jit(solution)/shard_map/psum | solution.py:82
  462.1 13.6 %psum.116 = f32[256]{0:T(256)S(1)} all-reduce(f32[256]{0:T(256)S(1)} %get-tuple-element.40), channel_id=1, replica_groups=mesh['sc'=4,'rows'=8] {'rows'}, use_global_device_ids=true, to_apply=%region_38.39 | all-reduce | flops 256 | bytes 2048 | tf_op jit(solution)/shard_map/psum | solution.py:82
  478.0 13.6 %psum.117 = f32[256]{0:T(256)S(1)} all-reduce(f32[256]{0:T(256)S(1)} %get-tuple-element.38), channel_id=1, replica_groups=mesh['sc'=4,'rows'=8] {'rows'}, use_global_device_ids=true, to_apply=%region_41.42 | all-reduce | flops 256 | bytes 2048 | tf_op jit(solution)/shard_map/psum | solution.py:82
  494.2 3.5 fusion.44
  497.7 3.6 all-to-all-start.2
  501.3 13.9 %psum.119 = f32[256]{0:T(256)S(1)} all-reduce(f32[256]{0:T(256)S(1)} %get-tuple-element.50), channel_id=1, replica_groups=mesh['sc'=4,'rows'=8] {'rows'}, use_global_device_ids=true, to_apply=%region_45.46 | all-reduce | flops 256 | bytes 2048 | tf_op jit(solution)/shard_map/psum | solution.py:95
  515.2 39.6 %all-reduce.12.cloned.1.call-done = f32[256,1024]{1,0:T(8,128)} async-done(((f32[256,1024]{1,0:T(8,128)}), f32[256,1024]{1,0:T(8,128)}) %all-reduce.12.cloned.1.call-update) | async-done | bytes 1048592 | tf_op jit(solution)/shard_map/psum | solution.py:95
  554.8 2.3 divide_bitcast_fusion
  557.2 5.0 gather_fusion.2
  (83 shorter events, 33.6 us)
Async XLA Ops:
  78.9 15.9 %all-to-all-start = ((s32[4,1,512]{2,1,0:T(1,128)}), s32[4,1,512]{2,1,0:T(1,128)S(1)}, u32[]{:S(2)}, u32[]{:S(2)}) async-start(s32[4,1,512]{2,1,0:T(1,128)} %bitcast.6), calls=%async_computation | async-start | bytes 16384 | tf_op jit(solution)/shard_map/all_to_all | solution.py:64
  94.8 7.0 %copy-start.8 = (s32[1,256]{1,0:T(1,128)S(1)}, s32[1,256]{1,0:T(1,128)}, u32[]{:S(2)}) copy-start(s32[1,256]{1,0:T(1,128)} %param.7) | copy-start | bytes 3076
  94.8 51.7 %all-to-all-start.1 = ((bf16[4,512,1024]{2,1,0:T(8,128)(2,1)}), bf16[4,512,1024]{2,1,0:T(8,128)(2,1)}, u32[]{:S(2)}, u32[]{:S(2)}) async-start(bf16[4,512,1024]{2,1,0:T(8,128)(2,1)} %bitcast.45), calls=%async_computation.1 | async-start | bytes 8388608 | tf_op jit(solution)/shard_map/all_to_all | solution.py:63
  99.8 227.1 %all-reduce.8.cloned.1.call-start = ((), (), s32[]{:S(2)}) async-start(), calls=%async_computation.3 | async-start | bytes 2097152 | tf_op jit(solution)/shard_map/psum | solution.py:91
  152.5 1.9 copy-start.6
  216.8 15.5 %copy-start.3 = (f32[2048,256]{1,0:T(8,128)}, f32[2048,256]{1,0:T(8,128)S(1)}, u32[]{:S(2)}) copy-start(f32[2048,256]{1,0:T(8,128)S(1)} %get-tuple-element.53) | copy-start | bytes 6291460
  250.0 15.7 %copy-start.4 = (f32[2048,256]{1,0:T(8,128)S(1)}, f32[2048,256]{1,0:T(8,128)}, u32[]{:S(2)}) copy-start(f32[2048,256]{1,0:T(8,128)} %get-tuple-element.47) | copy-start | bytes 6291460
  270.6 170.5 %all-reduce.10.cloned.1.call-start = ((), (), s32[]{:S(2)}) async-start(), calls=%async_computation.4 | async-start | bytes 2097152 | tf_op jit(solution)/shard_map/psum | solution.py:91
  331.8 14.0 %copy-start.1 = (f32[2048,256]{1,0:T(8,128)}, f32[2048,256]{1,0:T(8,128)S(1)}, u32[]{:S(2)}) copy-start(f32[2048,256]{1,0:T(8,128)S(1)} %get-tuple-element.55) | copy-start | bytes 6291460
  363.4 15.7 %copy-start.5 = (f32[2048,256]{1,0:T(8,128)S(1)}, f32[2048,256]{1,0:T(8,128)}, u32[]{:S(2)}) copy-start(f32[2048,256]{1,0:T(8,128)} %get-tuple-element.43) | copy-start | bytes 6291460
  384.1 170.8 %all-reduce.12.cloned.1.call-start = ((), (), s32[]{:S(2)}) async-start(), calls=%async_computation.5 | async-start | bytes 2097152 | tf_op jit(solution)/shard_map/psum | solution.py:95
  446.1 14.0 %copy-start.2 = (f32[2048,256]{1,0:T(8,128)}, f32[2048,256]{1,0:T(8,128)S(1)}, u32[]{:S(2)}) copy-start(f32[2048,256]{1,0:T(8,128)S(1)} %get-tuple-element.57) | copy-start | bytes 6291460
  462.1 14.0 %copy-start = (f32[2048,256]{1,0:T(8,128)}, f32[2048,256]{1,0:T(8,128)S(1)}, u32[]{:S(2)}) copy-start(f32[2048,256]{1,0:T(8,128)S(1)} %get-tuple-element.41) | copy-start | bytes 6291460
  491.6 2.6 copy-start.7
  497.7 59.5 %all-to-all-start.2 = ((bf16[4,512,256]{2,1,0:T(8,128)(2,1)}), bf16[4,512,256]{2,1,0:T(8,128)(2,1)S(1)}, u32[]{:S(2)}, u32[]{:S(2)}) async-start(bf16[4,512,256]{2,1,0:T(8,128)(2,1)} %bitcast.11), calls=%async_computation.2 | async-start | bytes 2097152 | tf_op jit(solution)/shard_map/all_to_all | solution.py:98
Sparse Core Ops, SparseCore 0:
  270.8 56.0 all-reduce.7
  384.2 56.9 all-reduce.9
  497.8 56.9 all-reduce.11
where the time goes:
time: 570 us; the launch traced here: 569 us
  blocking collectives  238 us (42%)
  waiting for transfers between devices  197 us (35%)
  local copies, waits for them, and re-layouts  44.2 us (8%)
  other arithmetic  35.6 us (6%)
  matrix products  25 us (4%)
  between operations  15.5 us (3%)
  starting transfers between devices  13.4 us (2%)
    psum x9, blocking collectives, on_device(): column = lax.psum(jnp.sum(plan, axis=0), 'rows')  124 us
    psum x2, waiting for transfers between devices, on_device(): mass = lax.psum(mass_part, 'rows')  113 us
    psum x1, blocking collectives, on_device(): cent = lax.psum(seeds, 'rows').astype(jnp.bfloat16)  57.9 us
    all_to_all x1, waiting for transfers between devices, on_device(): lax.all_to_all(outgoing, 'sc', split_axis=0, concat_axis=0, tiled=True)  44.5 us
    unnamed x1, blocking collectives  42 us
    psum x1, waiting for transfers between devices, on_device(): mass, weight = lax.psum((mass_part, weight_part), 'rows')  39.6 us
    gather x1, local copies, waits for them, and re-layouts, on_device(): out_rank = rank_pad[source].reshape(groups, slots)  20.6 us
    psum x1, blocking collectives, on_device(): mass, weight = lax.psum((mass_part, weight_part), 'rows')  13.9 us
  transfers between devices with their start and end apart: 6, of which 4 were waited for; matrix products, arithmetic and copies ran while one was open for 3% of the time, Pallas kernels for 0%

commit v1 on v0

v1 whole, which is shorter than its diff:
```python
import functools
import math

import jax
import jax.numpy as jnp
from jax import lax
from jax.experimental import pallas as pl
from jax.experimental.pallas import tpu as pltpu
from jax.sharding import PartitionSpec as P

ITERS = 3
ROUNDS = 3
MESH = pl.DeviceIdType.MESH
F32 = jnp.float32
BF16 = jnp.bfloat16


def kernel(
    G, R, tok, E, K, S, T,
    x_ref, labr_ref, labc_ref, init_ref,
    assign_ref, means_ref,
    xu, out, inc, plan, planb, lhst, acc, ret, target,
    cnt, cntr, cs, s1s, s1r, s2s, s2r, cent,
    d_ss, d_rs, c_ss, c_rs, k_ss, k_rs, cs_ss, cs_rs,
    s1_ss, s1_rs, s2_ss, s2_rs, g_ss, g_rs, f_ss, f_rs, r_ss, r_rs,
):
    g = lax.axis_index("sc")
    r = lax.axis_index("rows")
    Z = R // 2
    H = K // 2
    Q = H // Z
    N = G * S
    z = r // 2
    c = r % 2
    oc = 1 - c
    partner = z * 2 + oc

    def copy(src, dst, ss, rs, to):
        return pltpu.make_async_remote_copy(
            src_ref=src, dst_ref=dst, send_sem=ss, recv_sem=rs,
            device_id=to, device_id_type=MESH,
        )

    barrier = pltpu.get_barrier_semaphore()
    for off in range(1, R):
        pl.semaphore_signal(barrier, inc=1, device_id=(g, (r + off) % R), device_id_type=MESH)
    for off in range(1, G):
        pl.semaphore_signal(barrier, inc=1, device_id=((g + off) % G, r), device_id_type=MESH)

    def unit(i, carry):
        at = pl.ds(pl.multiple_of(i * 128, 128), 128)
        v = x_ref[at, :].astype(F32)
        scale = lax.rsqrt(jnp.mean(v * v, axis=1, keepdims=True) + 1e-05) * (1.0 / math.sqrt(E))
        xu[at, :] = (v * scale).astype(BF16)
        return carry

    lax.fori_loop(0, tok // 128, unit, 0)

    labr = labr_ref[...]
    labc = labc_ref[...]
    sub = lax.broadcasted_iota(jnp.int32, (tok, tok), 0)
    lane = lax.broadcasted_iota(jnp.int32, (tok, tok), 1)
    tri = jnp.where(sub < lane, 1.0, 0.0).astype(BF16)
    mem_r = jnp.where(lax.broadcasted_iota(jnp.int32, (16, tok), 0) == labr, 1.0, 0.0)
    before_r = jnp.dot(mem_r.astype(BF16), tri, preferred_element_type=F32)
    place_r = jnp.sum(before_r * mem_r, axis=0, keepdims=True)
    tri_l = jnp.where(sub > lane, 1.0, 0.0).astype(BF16)
    mem_c = jnp.where(lax.broadcasted_iota(jnp.int32, (tok, 128), 1) == labc, 1.0, 0.0)
    before_c = jnp.dot(tri_l, mem_c.astype(BF16), preferred_element_type=F32)
    place_c = jnp.sum(before_c * mem_c, axis=1, keepdims=True)
    target[...] = labc * S + place_c.astype(jnp.int32)
    place_i = place_r.astype(jnp.int32)
    cnt[g] = jnp.sum(mem_c, axis=0, keepdims=True)

    pl.semaphore_wait(barrier, R - 1 + G - 1)

    count_sends = []
    for off in range(1, G):
        to = (g + off) % G
        d = copy(cnt.at[g], cnt.at[g], c_ss.at[off], c_rs.at[g], (to, r))
        d.start()
        count_sends.append(d)

    DT = min(256, S)
    per = S // DT
    row_sends = []
    for off in range(1, G + 1):
        to = (g + off) % G
        chosen = jnp.where(labr == to, place_i, -1)
        for j in range(per):
            slot = lax.broadcasted_iota(jnp.int32, (DT, tok), 0) + j * DT
            perm = jnp.where(slot == chosen, 1.0, 0.0).astype(BF16)
            block = jnp.dot(perm, xu[...], preferred_element_type=F32).astype(BF16)
            if off < G:
                out[off - 1, pl.ds(j * DT, DT), :] = block
                d = copy(
                    out.at[off - 1, pl.ds(j * DT, DT), :],
                    inc.at[g, pl.ds(j * DT, DT), :],
                    d_ss.at[off * per + j], d_rs.at[g * per + j], (to, r),
                )
                d.start()
                row_sends.append(d)
            else:
                inc[g, pl.ds(j * DT, DT), :] = block

    for off in range(1, G):
        src = (g + off) % G
        copy(cnt.at[src], cnt.at[src], c_ss.at[off], c_rs.at[src], (src, r)).wait_recv()
    lanes = lax.broadcasted_iota(jnp.int32, (1, 128), 1)
    mine = jnp.zeros((1, 128), F32)
    n_here = []
    for q in range(G):
        n_q = jnp.sum(jnp.where(lanes == g, cnt[q], 0.0), axis=1, keepdims=True)
        n_here.append(n_q)
        mine = mine + jnp.where(lanes == q, n_q, 0.0)
    cntr[r] = mine
    rank_sends = []
    for off in range(1, R):
        to = (r + off) % R
        d = copy(cntr.at[r], cntr.at[r], k_ss.at[off], k_rs.at[r], (g, to))
        d.start()
        rank_sends.append(d)
    for off in range(1, R):
        src = (r + off) % R
        copy(cntr.at[src], cntr.at[src], k_ss.at[off], k_rs.at[src], (g, src)).wait_recv()
    total = jnp.zeros((1, 128), F32)
    early = jnp.zeros((1, 128), F32)
    for q in range(R):
        row = cntr[q]
        total = total + row
        early = early + jnp.where(r > q, row, 0.0)
    count = jnp.sum(total, axis=1, keepdims=True)
    asked = init_ref[...].astype(F32)
    wanted = asked - jnp.floor((asked + 0.5) / count) * count
    slots = lax.broadcasted_iota(jnp.int32, (1, S), 1).astype(F32)
    for q in range(G):
        base = jnp.sum(
            jnp.where(lanes < q, total, 0.0) + jnp.where(lanes == q, early, 0.0),
            axis=1, keepdims=True,
        )
        rank = jnp.where(slots < n_here[q], slots + base, -1.0)
        pick = jnp.where(wanted == rank, 1.0, 0.0).astype(BF16)
        lhst[0, :, pl.ds(q * S, S)] = pick[:H]
        lhst[1, :, pl.ds(q * S, S)] = pick[H:]

    for off in range(1, G):
        src = (g + off) % G
        for j in range(per):
            part = inc.at[src, pl.ds(j * DT, DT), :]
            copy(part, part, d_ss.at[off * per + j], d_rs.at[src * per + j], (src, r)).wait_recv()

    def half_sum(h):
        def one(q, carry):
            at = pl.ds(pl.multiple_of(q * S, S), S)
            acc[...] += jnp.dot(lhst[h, :, at], inc[q], preferred_element_type=F32)
            return carry

        acc[...] = jnp.zeros_like(acc)
        lax.fori_loop(0, G, one, 0)

    def big(t, finish, meanwhile=None):
        slot = t % 2
        half_sum(oc)
        s1s[...] = acc[...].astype(BF16)
        d1 = copy(s1s, s1r.at[slot], s1_ss.at[slot], s1_rs.at[slot], (g, partner))
        d1.start()
        half_sum(c)
        d1.wait()
        acc[...] += s1r[slot].astype(F32)
        for p in range(Z):
            s2s[p] = acc[pl.ds(p * Q, Q), :].astype(BF16)
        sends = []
        for off in range(1, Z):
            to = (z + off) % Z
            d = copy(s2s.at[to], s2r.at[slot, z], s2_ss.at[slot, off], s2_rs.at[slot, z], (g, to * 2 + c))
            d.start()
            sends.append(d)
        if meanwhile is not None:
            meanwhile()
        own = acc[pl.ds(pl.multiple_of(z * Q, Q), Q), :]
        for off in range(1, Z):
            src = (z + off) % Z
            part = s2r.at[slot, src]
            copy(part, part, s2_ss.at[slot, off], s2_rs.at[slot, src], (g, src * 2 + c)).wait_recv()
            own = own + s2r[slot, src].astype(F32)
        cent[slot, c, z] = finish(own).astype(BF16)
        for off in range(1, Z):
            to = (z + off) % Z
            d = copy(cent.at[slot, c, z], cent.at[slot, c, z], g_ss.at[slot, off], g_rs.at[slot, z], (g, to * 2 + c))
            d.start()
            sends.append(d)
        d = copy(cent.at[slot, c, z], cent.at[slot, c, z], f_ss.at[slot, z], f_rs.at[slot, z], (g, partner))
        d.start()
        sends.append(d)
        for off in range(1, Z):
            src = (z + off) % Z
            part = cent.at[slot, c, src]
            copy(part, part, g_ss.at[slot, off], g_rs.at[slot, src], (g, src * 2 + c)).wait_recv()
            d = copy(part, part, f_ss.at[slot, src], f_rs.at[slot, src], (g, partner))
            d.start()
            sends.append(d)
        for off in range(Z):
            src = (z + off) % Z
            part = cent.at[slot, oc, src]
            copy(part, part, f_ss.at[slot, src], f_rs.at[slot, src], (g, partner)).wait_recv()
        for d in sends:
            d.wait_send()

    def column_sum(t, part8):
        slot = t % 2
        cs[slot, r] = jnp.sum(part8, axis=0, keepdims=True)
        sends = []
        for off in range(1, R):
            to = (r + off) % R
            d = copy(cs.at[slot, r], cs.at[slot, r], cs_ss.at[slot, off], cs_rs.at[slot, r], (g, to))
            d.start()
            sends.append(d)
        for off in range(1, R):
            src = (r + off) % R
            part = cs.at[slot, src]
            copy(part, part, cs_ss.at[slot, off], cs_rs.at[slot, src], (g, src)).wait_recv()
        whole = cs[slot, 0]
        for q in range(1, R):
            whole = whole + cs[slot, q]
        for d in sends:
            d.wait_send()
        return whole

    tiles = N // T
    zero8 = jnp.zeros((8, K), F32)

    def down(v):
        return jnp.sum(v.reshape(T // 8, 8, K), axis=0)

    def assign_rows():
        for off in range(1, G):
            src = (g + off) % G
            part = ret.at[src]
            copy(part, part, r_ss.at[off], r_rs.at[src], (src, r)).wait_recv()

        def one(i, carry):
            at = pl.ds(pl.multiple_of(i * 256, 256), 256)
            hot = jnp.where(
                lax.broadcasted_iota(jnp.int32, (256, N), 1) == target[at, :], 1.0, 0.0
            ).astype(BF16)
            assign_ref[at, :] = jnp.dot(
                hot, ret[...].reshape(N, K), preferred_element_type=F32
            ).astype(BF16)
            return carry

        lax.fori_loop(0, tok // 256, one, 0)

    big(0, lambda v: v)
    step = 0
    back_sends = []
    for round_index in range(ROUNDS):
        last = round_index == ROUNDS - 1
        slot = round_index % 2
        part = zero8
        for q in range(G):
            n_q = n_here[q]

            def score(j, part, q=q, n_q=n_q):
                first = j * T
                v = lax.dot_general(
                    inc[q, pl.ds(pl.multiple_of(first, T), T), :],
                    cent[slot].reshape(K, E),
                    (((1,), (1,)), ((), ())), preferred_element_type=F32,
                )
                at = (lax.broadcasted_iota(jnp.int32, (T, 1), 0) + first).astype(F32)
                v = jnp.where(at < n_q, jnp.exp(v * 10.0), 0.0)
                plan[pl.ds(pl.multiple_of(q * S + first, T), T), :] = v
                return part + down(v)

            part = lax.fori_loop(0, S // T, score, part)
        for it in range(ITERS):
            col = 1.0 / column_sum(step, part)
            step += 1
            if it < ITERS - 1:

                def sweep(i, part, col=col):
                    v = plan[pl.ds(pl.multiple_of(i * T, T), T), :]
                    s = jnp.sum(v * col, axis=1, keepdims=True)
                    return part + down(v * jnp.where(s > 0.0, 1.0 / s, 0.0))

                part = lax.fori_loop(0, tiles, sweep, zero8)
            else:

                def settle(i, part, col=col):
                    at = pl.ds(pl.multiple_of(i * T, T), T)
                    v = plan[at, :] * col
                    s = jnp.sum(v, axis=1, keepdims=True)
                    v = v * jnp.where(s > 0.0, 1.0 / s, 0.0)
                    if last:
                        planb[at, :] = v.astype(BF16)
                    vt = v.T.astype(BF16)
                    lhst[0, :, at] = vt[:H]
                    lhst[1, :, at] = vt[H:]
                    return part + down(v)

                part = lax.fori_loop(0, tiles, settle, zero8)
        if not last:
            big(
                round_index + 1,
                lambda v: v * lax.rsqrt(jnp.sum(v * v, axis=1, keepdims=True) + 1e-06),
            )
        else:
            for off in range(1, G):
                to = (g + off) % G
                d = copy(
                    planb.at[pl.ds(pl.multiple_of(to * S, S), S), :], ret.at[g],
                    r_ss.at[off], r_rs.at[g], (to, r),
                )
                d.start()
                back_sends.append(d)
            ret[g] = planb[pl.ds(pl.multiple_of(g * S, S), S), :]
            weight = column_sum(step, part)
            first = c * H + z * Q
            wide = lax.broadcasted_iota(jnp.int32, (Q, K), 0) + first
            pick = wide == lax.broadcasted_iota(jnp.int32, (Q, K), 1)
            w = jnp.sum(jnp.where(pick, weight, 0.0), axis=1, keepdims=True)
            big(ROUNDS, lambda v: v / w, assign_rows)
            means_ref[...] = cent[ROUNDS % 2].reshape(K, E).astype(F32)

    for d in count_sends + row_sends + rank_sends + back_sends:
        d.wait_send()


def on_device(G, R, embeddings, labels, init_idx):
    tok, E = embeddings.shape
    K = init_idx.shape[1]
    S = 2 * tok // G
    T = min(256, S)
    N = G * S
    Z = R // 2
    Q = K // 2 // Z
    per = S // min(256, S)
    dma = pltpu.SemaphoreType.DMA
    vm = pltpu.VMEM
    assign, means = pl.pallas_call(
        functools.partial(kernel, G, R, tok, E, K, S, T),
        out_shape=(
            jax.ShapeDtypeStruct((tok, K), BF16),
            jax.ShapeDtypeStruct((K, E), F32),
        ),
        in_specs=[pl.BlockSpec(memory_space=pltpu.VMEM)] * 4,
        out_specs=[pl.BlockSpec(memory_space=pltpu.VMEM)] * 2,
        scratch_shapes=[
            vm((tok, E), BF16),
            vm((G - 1, S, E), BF16),
            vm((G, S, E), BF16),
            vm((N, K), F32),
            vm((N, K), BF16),
            vm((2, K // 2, N), BF16),
            vm((K // 2, E), F32),
            vm((G, S, K), BF16),
            vm((tok, 1), jnp.int32),
            vm((G, 1, 128), F32),
            vm((R, 1, 128), F32),
            vm((2, R, 1, K), F32),
            vm((K // 2, E), BF16),
            vm((2, K // 2, E), BF16),
            vm((Z, Q, E), BF16),
            vm((2, Z, Q, E), BF16),
            vm((2, 2, Z, Q, E), BF16),
            dma(((G + 1) * per,)), dma((G * per,)),
            dma((G,)), dma((G,)),
            dma((R,)), dma((R,)),
            dma((2, R)), dma((2, R)),
            dma((2,)), dma((2,)),
            dma((2, Z)), dma((2, Z)),
            dma((2, Z)), dma((2, Z)),
            dma((2, Z)), dma((2, Z)),
            dma((G,)), dma((G,)),
        ],
        compiler_params=pltpu.CompilerParams(
            collective_id=0, has_side_effects=True, vmem_limit_bytes=48 * 1024 * 1024,
        ),
    )(embeddings, labels.reshape(1, tok), labels, init_idx.reshape(K, 1))
    return (assign, means[None])


def solution(mesh):
    return jax.shard_map(
        functools.partial(on_device, mesh.shape["sc"], mesh.shape["rows"]),
        mesh=mesh,
        in_specs=(P(("sc", "rows"), None), P(("sc", "rows"), None), P("sc", None)),
        out_specs=(P(("sc", "rows"), None), P("sc", None, None)),
        check_vma=False,
    )
```

time: 570 us -> 191 us (0.34)
  blocking collectives: 238 us -> 0 us
  waiting for transfers between devices: 197 us -> 0 us
  Pallas kernels: 0 us -> 184 us
  local copies, waits for them, and re-layouts: 44.2 us -> 5.75 us
  other arithmetic: 35.6 us -> 0 us
  matrix products: 25 us -> 0 us
  between operations: 15.5 us -> 0.66 us
  starting transfers between devices: 13.4 us -> 0 us
    psum x11 -> x0, blocking collectives: 196 us -> none  [the longest x9 124 us: on_device(): column = lax.psum(jnp.sum(plan, axis=0), 'rows')]
    pallas_call x0 -> x1, Pallas kernels: none -> 184 us  [on_device(): pl.pallas_call(functools.partial(kernel, G, R, tok, E, K, S, T), out_shap...]
    psum x3 -> x0, waiting for transfers between devices: 153 us -> none  [the longest x2 113 us: on_device(): mass = lax.psum(mass_part, 'rows')]
    all_to_all x3 -> x0, waiting for transfers between devices: 44.6 us -> none  [the longest x1 44.5 us: on_device(): lax.all_to_all(outgoing, 'sc', split_axis=0, concat_axis=0, tiled=True)]
    unnamed x1 -> x0, blocking collectives: 42 us -> none
    gather x3 -> x0, local copies, waits for them, and re-layouts: 35.2 us -> none  [the longest x1 20.6 us: on_device(): out_rank = rank_pad[source].reshape(groups, slots)]
    reduce_sum x22 -> x0, other arithmetic: 27.2 us -> none  [the longest x6 11.3 us: on_device(): column = lax.psum(jnp.sum(plan, axis=0), 'rows')]
    dot_general x7 -> x0, matrix products: 25 us -> none  [the longest x3 13.3 us: on_device(): lax.dot_general(plan_b, members, contract_rows, preferred_element_type=jn...]
  transfers between devices with their start and end apart: 6 -> 0, of which waited for: 4 -> 0; matrix products, arithmetic and copies ran while one was open for 3% -> 0% of each run, Pallas kernels for 0% -> 0%
where the time goes in v1:
time: 191 us
  Pallas kernels  184 us (96%)
  local copies, waits for them, and re-layouts  5.75 us (3%)
    pallas_call x1, Pallas kernels, on_device(): pl.pallas_call(functools.partial(kernel, G, R, tok, E, K, S, T), out_shap...  184 us
    unnamed x7, local copies, waits for them, and re-layouts  4.95 us

profile of v1, /device:TPU:0, one launch (start us, length us, event | category | flops | bytes accessed | tf_op | source)
XLA Modules:
  0.0 190.7 jit_solution(941828154058749788)
XLA Ops:
  0.6 0.8 copy.7.init_ref
  1.4 0.9 copy.6.labc_ref
  2.4 0.0 copy-start
  2.4 1.6 copy-done
  4.0 0.0 copy-start.1
  4.0 0.7 copy-done.1
  4.6 184.3 %shard_map.50 = (bf16[1024,256]{1,0:T(8,128)(2,1)S(1)}, f32[256,1024]{1,0:T(8,128)S(1)}) custom-call(bf16[1024,1024]{1,0:T(8,128)(2,1)S(1)} %copy-done, s32[1,1024]{1,0:T(1,128)S(1)} %bitcast.4, s32[1024,1]{1,0:T(8,128)S(1)} %copy.6.labc_ref, s32[256,1]{1,0:T(8,128)S(1)} %copy.7.init_ref), custom_call_target="tpu_custom_call" | custom-call | tf_op jit(solution)/shard_map/pallas_call | solution.py:340
  188.9 0.8 copy.10
  189.7 1.0 copy.11
Async XLA Ops:
  2.4 1.6 copy-start
  4.0 0.7 copy-start.1

commit v2 on v1

--- a/solution.py
+++ b/solution.py
@@ -17,7 +17,7 @@
 
 def kernel(
     G, R, tok, E, K, S, T,
-    x_ref, labr_ref, labc_ref, init_ref,
+    x_ref, labr_ref, init_ref,
     assign_ref, means_ref,
     xu, out, inc, plan, planb, lhst, acc, ret, target,
     cnt, cntr, cs, s1s, s1r, s2s, s2r, cent,
@@ -57,20 +57,19 @@
     lax.fori_loop(0, tok // 128, unit, 0)
 
     labr = labr_ref[...]
-    labc = labc_ref[...]
-    sub = lax.broadcasted_iota(jnp.int32, (tok, tok), 0)
-    lane = lax.broadcasted_iota(jnp.int32, (tok, tok), 1)
+    sub = lax.broadcasted_iota(jnp.int32, (128, 128), 0)
+    lane = lax.broadcasted_iota(jnp.int32, (128, 128), 1)
     tri = jnp.where(sub < lane, 1.0, 0.0).astype(BF16)
-    mem_r = jnp.where(lax.broadcasted_iota(jnp.int32, (16, tok), 0) == labr, 1.0, 0.0)
-    before_r = jnp.dot(mem_r.astype(BF16), tri, preferred_element_type=F32)
-    place_r = jnp.sum(before_r * mem_r, axis=0, keepdims=True)
-    tri_l = jnp.where(sub > lane, 1.0, 0.0).astype(BF16)
-    mem_c = jnp.where(lax.broadcasted_iota(jnp.int32, (tok, 128), 1) == labc, 1.0, 0.0)
-    before_c = jnp.dot(tri_l, mem_c.astype(BF16), preferred_element_type=F32)
-    place_c = jnp.sum(before_c * mem_c, axis=1, keepdims=True)
-    target[...] = labc * S + place_c.astype(jnp.int32)
-    place_i = place_r.astype(jnp.int32)
-    cnt[g] = jnp.sum(mem_c, axis=0, keepdims=True)
+    mem = jnp.where(lax.broadcasted_iota(jnp.int32, (16, tok), 0) == labr, 1.0, 0.0)
+    seen = jnp.zeros((16, 1), F32)
+    places = []
+    for b in range(tok // 128):
+        part = mem[:, b * 128:(b + 1) * 128]
+        before = jnp.dot(part.astype(BF16), tri, preferred_element_type=F32) + seen
+        places.append(jnp.sum(before * part, axis=0, keepdims=True))
+        seen = seen + jnp.sum(part, axis=1, keepdims=True)
+    place_i = jnp.concatenate(places, axis=1).astype(jnp.int32)
+    cnt[g] = jnp.sum(jnp.where(sub[:16] == lane[:16], seen, 0.0), axis=0, keepdims=True)
 
     pl.semaphore_wait(barrier, R - 1 + G - 1)
 
@@ -102,6 +101,11 @@
                 row_sends.append(d)
             else:
                 inc[g, pl.ds(j * DT, DT), :] = block
+
+    slot_of = (labr * S + place_i).astype(F32)
+    for b in range(tok // 128):
+        wide = jnp.broadcast_to(slot_of[:, b * 128:(b + 1) * 128], (128, 128))
+        target[pl.ds(b * 128, 128), :] = wide.T[:, :1].astype(jnp.int32)
 
     for off in range(1, G):
         src = (g + off) % G
@@ -149,40 +153,47 @@
             part = inc.at[src, pl.ds(j * DT, DT), :]
             copy(part, part, d_ss.at[off * per + j], d_rs.at[src * per + j], (src, r)).wait_recv()
 
-    def half_sum(h):
-        def one(q, carry):
-            at = pl.ds(pl.multiple_of(q * S, S), S)
-            acc[...] += jnp.dot(lhst[h, :, at], inc[q], preferred_element_type=F32)
-            return carry
-
-        acc[...] = jnp.zeros_like(acc)
-        lax.fori_loop(0, G, one, 0)
+    C = E // 2
+
+    def half_sum(h, e):
+        rows = inc[:, :, pl.ds(e * C, C)].reshape(N, C)
+        return jnp.dot(lhst[h], rows, preferred_element_type=F32)
 
     def big(t, finish, meanwhile=None):
         slot = t % 2
-        half_sum(oc)
-        s1s[...] = acc[...].astype(BF16)
-        d1 = copy(s1s, s1r.at[slot], s1_ss.at[slot], s1_rs.at[slot], (g, partner))
-        d1.start()
-        half_sum(c)
-        d1.wait()
-        acc[...] += s1r[slot].astype(F32)
-        for p in range(Z):
-            s2s[p] = acc[pl.ds(p * Q, Q), :].astype(BF16)
+        first = []
         sends = []
-        for off in range(1, Z):
-            to = (z + off) % Z
-            d = copy(s2s.at[to], s2r.at[slot, z], s2_ss.at[slot, off], s2_rs.at[slot, z], (g, to * 2 + c))
+        for e in range(2):
+            s1s[e] = half_sum(oc, e).astype(BF16)
+            d = copy(s1s.at[e], s1r.at[slot, e], s1_ss.at[slot, e], s1_rs.at[slot, e], (g, partner))
             d.start()
-            sends.append(d)
-        if meanwhile is not None:
-            meanwhile()
-        own = acc[pl.ds(pl.multiple_of(z * Q, Q), Q), :]
-        for off in range(1, Z):
-            src = (z + off) % Z
-            part = s2r.at[slot, src]
-            copy(part, part, s2_ss.at[slot, off], s2_rs.at[slot, src], (g, src * 2 + c)).wait_recv()
-            own = own + s2r[slot, src].astype(F32)
+            first.append(d)
+        for e in range(2):
+            acc[e] = half_sum(c, e)
+            first[e].wait_recv()
+            acc[e] += s1r[slot, e].astype(F32)
+            for p in range(Z):
+                s2s[e, p] = acc[e, pl.ds(p * Q, Q), :].astype(BF16)
+            for off in range(1, Z):
+                to = (z + off) % Z
+                d = copy(
+                    s2s.at[e, to], s2r.at[slot, e, z],
+                    s2_ss.at[slot, e, off], s2_rs.at[slot, e, z], (g, to * 2 + c),
+                )
+                d.start()
+                sends.append(d)
+        halves = []
+        for e in range(2):
+            own = acc[e, pl.ds(pl.multiple_of(z * Q, Q), Q), :]
+            for off in range(1, Z):
+                src = (z + off) % Z
+                part = s2r.at[slot, e, src]
+                copy(
+                    part, part, s2_ss.at[slot, e, off], s2_rs.at[slot, e, src], (g, src * 2 + c)
+                ).wait_recv()
+                own = own + s2r[slot, e, src].astype(F32)
+            halves.append(own)
+        own = jnp.concatenate(halves, axis=1)
         cent[slot, c, z] = finish(own).astype(BF16)
         for off in range(1, Z):
             to = (z + off) % Z
@@ -199,11 +210,13 @@
             d = copy(part, part, f_ss.at[slot, src], f_rs.at[slot, src], (g, partner))
             d.start()
             sends.append(d)
+        if meanwhile is not None:
+            meanwhile()
         for off in range(Z):
             src = (z + off) % Z
             part = cent.at[slot, oc, src]
             copy(part, part, f_ss.at[slot, src], f_rs.at[slot, src], (g, partner)).wait_recv()
-        for d in sends:
+        for d in first + sends:
             d.wait_send()
 
     def column_sum(t, part8):
@@ -343,7 +356,7 @@
             jax.ShapeDtypeStruct((tok, K), BF16),
             jax.ShapeDtypeStruct((K, E), F32),
         ),
-        in_specs=[pl.BlockSpec(memory_space=pltpu.VMEM)] * 4,
+        in_specs=[pl.BlockSpec(memory_space=pltpu.VMEM)] * 3,
         out_specs=[pl.BlockSpec(memory_space=pltpu.VMEM)] * 2,
         scratch_shapes=[
             vm((tok, E), BF16),
@@ -352,23 +365,23 @@
             vm((N, K), F32),
             vm((N, K), BF16),
             vm((2, K // 2, N), BF16),
-            vm((K // 2, E), F32),
+            vm((2, K // 2, E // 2), F32),
             vm((G, S, K), BF16),
             vm((tok, 1), jnp.int32),
             vm((G, 1, 128), F32),
             vm((R, 1, 128), F32),
             vm((2, R, 1, K), F32),
-            vm((K // 2, E), BF16),
-            vm((2, K // 2, E), BF16),
-            vm((Z, Q, E), BF16),
-            vm((2, Z, Q, E), BF16),
+            vm((2, K // 2, E // 2), BF16),
+            vm((2, 2, K // 2, E // 2), BF16),
+            vm((2, Z, Q, E // 2), BF16),
+            vm((2, 2, Z, Q, E // 2), BF16),
             vm((2, 2, Z, Q, E), BF16),
             dma(((G + 1) * per,)), dma((G * per,)),
             dma((G,)), dma((G,)),
             dma((R,)), dma((R,)),
             dma((2, R)), dma((2, R)),
-            dma((2,)), dma((2,)),
-            dma((2, Z)), dma((2, Z)),
+            dma((2, 2)), dma((2, 2)),
+            dma((2, 2, Z)), dma((2, 2, Z)),
             dma((2, Z)), dma((2, Z)),
             dma((2, Z)), dma((2, Z)),
             dma((G,)), dma((G,)),
@@ -376,7 +389,7 @@
         compiler_params=pltpu.CompilerParams(
             collective_id=0, has_side_effects=True, vmem_limit_bytes=48 * 1024 * 1024,
         ),
-    )(embeddings, labels.reshape(1, tok), labels, init_idx.reshape(K, 1))
+    )(embeddings, labels.reshape(1, tok), init_idx.reshape(K, 1))
     return (assign, means[None])
 
 

time: 191 us -> 185 us (0.969)
  Pallas kernels: 184 us -> 179 us
    pallas_call x1, Pallas kernels: 184 us -> 179 us  [on_device(): pl.pallas_call(functools.partial(kernel, G, R, tok, E, K, S, T), out_shap...]
    unnamed x7 -> x6, local copies, waits for them, and re-layouts: 4.95 us -> 4.04 us
where the time goes in v2:
time: 185 us
  Pallas kernels  179 us (97%)
  local copies, waits for them, and re-layouts  4.85 us (3%)
    pallas_call x1, Pallas kernels, on_device(): pl.pallas_call(functools.partial(kernel, G, R, tok, E, K, S, T), out_shap...  179 us
    unnamed x6, local copies, waits for them, and re-layouts  4.04 us

profile of v2, /device:TPU:0, one launch (start us, length us, event | category | flops | bytes accessed | tf_op | source)
XLA Modules:
  0.0 184.8 jit_solution(13484407634251007803)
XLA Ops:
  0.6 0.8 copy.5.init_ref
  1.4 0.0 copy-start
  1.5 1.6 copy-done
  3.0 0.0 copy-start.1
  3.0 0.7 copy-done.1
  3.7 179.3 %shard_map.50 = (bf16[1024,256]{1,0:T(8,128)(2,1)S(1)}, f32[256,1024]{1,0:T(8,128)S(1)}) custom-call(bf16[1024,1024]{1,0:T(8,128)(2,1)S(1)} %copy-done, s32[1,1024]{1,0:T(1,128)S(1)} %bitcast.4, s32[256,1]{1,0:T(8,128)S(1)} %copy.5.init_ref), custom_call_target="tpu_custom_call" | custom-call | tf_op jit(solution)/shard_map/pallas_call | solution.py:353
  183.0 0.8 copy.8
  183.8 1.0 copy.9
Async XLA Ops:
  1.4 1.6 copy-start
  3.0 0.7 copy-start.1

commit v3 on v2

--- a/solution.py
+++ b/solution.py
@@ -80,27 +80,25 @@
         d.start()
         count_sends.append(d)
 
-    DT = min(256, S)
+    DT = min(128, S)
     per = S // DT
     row_sends = []
-    for off in range(1, G + 1):
-        to = (g + off) % G
-        chosen = jnp.where(labr == to, place_i, -1)
-        for j in range(per):
-            slot = lax.broadcasted_iota(jnp.int32, (DT, tok), 0) + j * DT
-            perm = jnp.where(slot == chosen, 1.0, 0.0).astype(BF16)
-            block = jnp.dot(perm, xu[...], preferred_element_type=F32).astype(BF16)
-            if off < G:
-                out[off - 1, pl.ds(j * DT, DT), :] = block
-                d = copy(
-                    out.at[off - 1, pl.ds(j * DT, DT), :],
-                    inc.at[g, pl.ds(j * DT, DT), :],
-                    d_ss.at[off * per + j], d_rs.at[g * per + j], (to, r),
-                )
-                d.start()
-                row_sends.append(d)
-            else:
-                inc[g, pl.ds(j * DT, DT), :] = block
+    chosen = [jnp.where(labr == (g + off) % G, place_i, -1) for off in range(1, G + 1)]
+    for j, off in [(j, off) for j in range(per) for off in range(1, G)] + [(j, G) for j in range(per)]:
+        at = pl.ds(j * DT, DT)
+        slot = lax.broadcasted_iota(jnp.int32, (DT, tok), 0) + j * DT
+        perm = jnp.where(slot == chosen[off - 1], 1.0, 0.0).astype(BF16)
+        block = jnp.dot(perm, xu[...], preferred_element_type=F32).astype(BF16)
+        if off < G:
+            out[off - 1, at, :] = block
+            d = copy(
+                out.at[off - 1, at, :], inc.at[g, at, :],
+                d_ss.at[off * per + j], d_rs.at[g * per + j], ((g + off) % G, r),
+            )
+            d.start()
+            row_sends.append(d)
+        else:
+            inc[g, at, :] = block
 
     slot_of = (labr * S + place_i).astype(F32)
     for b in range(tok // 128):
@@ -203,6 +201,8 @@
         d = copy(cent.at[slot, c, z], cent.at[slot, c, z], f_ss.at[slot, z], f_rs.at[slot, z], (g, partner))
         d.start()
         sends.append(d)
+        if meanwhile is not None:
+            meanwhile()
         for off in range(1, Z):
             src = (z + off) % Z
             part = cent.at[slot, c, src]
@@ -210,8 +210,6 @@
             d = copy(part, part, f_ss.at[slot, src], f_rs.at[slot, src], (g, partner))
             d.start()
             sends.append(d)
-        if meanwhile is not None:
-            meanwhile()
         for off in range(Z):
             src = (z + off) % Z
             part = cent.at[slot, oc, src]
@@ -219,7 +217,7 @@
         for d in first + sends:
             d.wait_send()
 
-    def column_sum(t, part8):
+    def column_start(t, part8):
         slot = t % 2
         cs[slot, r] = jnp.sum(part8, axis=0, keepdims=True)
         sends = []
@@ -228,6 +226,10 @@
             d = copy(cs.at[slot, r], cs.at[slot, r], cs_ss.at[slot, off], cs_rs.at[slot, r], (g, to))
             d.start()
             sends.append(d)
+        return sends
+
+    def column_sum(t, sends):
+        slot = t % 2
         for off in range(1, R):
             src = (r + off) % R
             part = cs.at[slot, src]
@@ -287,7 +289,7 @@
 
             part = lax.fori_loop(0, S // T, score, part)
         for it in range(ITERS):
-            col = 1.0 / column_sum(step, part)
+            col = 1.0 / column_sum(step, column_start(step, part))
             step += 1
             if it < ITERS - 1:
 
@@ -327,12 +329,15 @@
                 d.start()
                 back_sends.append(d)
             ret[g] = planb[pl.ds(pl.multiple_of(g * S, S), S), :]
-            weight = column_sum(step, part)
-            first = c * H + z * Q
-            wide = lax.broadcasted_iota(jnp.int32, (Q, K), 0) + first
-            pick = wide == lax.broadcasted_iota(jnp.int32, (Q, K), 1)
-            w = jnp.sum(jnp.where(pick, weight, 0.0), axis=1, keepdims=True)
-            big(ROUNDS, lambda v: v / w, assign_rows)
+            weight_sends = column_start(step, part)
+
+            def mean_of(v):
+                weight = column_sum(step, weight_sends)
+                wide = lax.broadcasted_iota(jnp.int32, (Q, K), 0) + (c * H + z * Q)
+                pick = wide == lax.broadcasted_iota(jnp.int32, (Q, K), 1)
+                return v / jnp.sum(jnp.where(pick, weight, 0.0), axis=1, keepdims=True)
+
+            big(ROUNDS, mean_of, assign_rows)
             means_ref[...] = cent[ROUNDS % 2].reshape(K, E).astype(F32)
 
     for d in count_sends + row_sends + rank_sends + back_sends:
@@ -347,7 +352,7 @@
     N = G * S
     Z = R // 2
     Q = K // 2 // Z
-    per = S // min(256, S)
+    per = S // min(128, S)
     dma = pltpu.SemaphoreType.DMA
     vm = pltpu.VMEM
     assign, means = pl.pallas_call(

time: 185 us -> 181 us (0.978)
  Pallas kernels: 179 us -> 175 us
    pallas_call x1, Pallas kernels: 179 us -> 175 us  [on_device(): pl.pallas_call(functools.partial(kernel, G, R, tok, E, K, S, T), out_shap...]
where the time goes in v3:
time: 181 us; the launch traced here: 180 us
  Pallas kernels  175 us (97%)
  local copies, waits for them, and re-layouts  4.85 us (3%)
    pallas_call x1, Pallas kernels, on_device(): pl.pallas_call(functools.partial(kernel, G, R, tok, E, K, S, T), out_shap...  175 us
    unnamed x6, local copies, waits for them, and re-layouts  4.04 us

profile of v3, /device:TPU:0, one launch (start us, length us, event | category | flops | bytes accessed | tf_op | source)
XLA Modules:
  0.0 180.4 jit_solution(9330111852131391296)
XLA Ops:
  0.6 0.8 copy.5.init_ref
  1.4 0.0 copy-start
  1.5 1.6 copy-done
  3.0 0.0 copy-start.1
  3.0 0.7 copy-done.1
  3.7 174.9 %shard_map.50 = (bf16[1024,256]{1,0:T(8,128)(2,1)S(1)}, f32[256,1024]{1,0:T(8,128)S(1)}) custom-call(bf16[1024,1024]{1,0:T(8,128)(2,1)S(1)} %copy-done, s32[1,1024]{1,0:T(1,128)S(1)} %bitcast.4, s32[256,1]{1,0:T(8,128)S(1)} %copy.5.init_ref), custom_call_target="tpu_custom_call" | custom-call | tf_op jit(solution)/shard_map/pallas_call | solution.py:358
  178.6 0.8 copy.8
  179.4 1.0 copy.9
Async XLA Ops:
  1.4 1.6 copy-start
  3.0 0.7 copy-start.1

commit v4 on v3

--- a/solution.py
+++ b/solution.py
@@ -221,7 +221,7 @@
         slot = t % 2
         cs[slot, r] = jnp.sum(part8, axis=0, keepdims=True)
         sends = []
-        for off in range(1, R):
+        for off in sorted(range(1, R), key=lambda o: -min(o, R - o)):
             to = (r + off) % R
             d = copy(cs.at[slot, r], cs.at[slot, r], cs_ss.at[slot, off], cs_rs.at[slot, r], (g, to))
             d.start()

time: 181 us -> 181 us (level)
  no operation moved by 1% of the time
where the time goes in v4:
time: 181 us; the launch traced here: 180 us
  Pallas kernels  175 us (97%)
  local copies, waits for them, and re-layouts  4.85 us (3%)
    pallas_call x1, Pallas kernels, on_device(): pl.pallas_call(functools.partial(kernel, G, R, tok, E, K, S, T), out_shap...  175 us
    unnamed x6, local copies, waits for them, and re-layouts  4.04 us

profile of v4, /device:TPU:0, one launch (start us, length us, event | category | flops | bytes accessed | tf_op | source)
XLA Modules:
  0.0 180.4 jit_solution(4209299189910961166)
XLA Ops:
  0.6 0.8 copy.5.init_ref
  1.4 0.0 copy-start
  1.5 1.6 copy-done
  3.0 0.0 copy-start.1
  3.0 0.7 copy-done.1
  3.7 174.9 %shard_map.50 = (bf16[1024,256]{1,0:T(8,128)(2,1)S(1)}, f32[256,1024]{1,0:T(8,128)S(1)}) custom-call(bf16[1024,1024]{1,0:T(8,128)(2,1)S(1)} %copy-done, s32[1,1024]{1,0:T(1,128)S(1)} %bitcast.4, s32[256,1]{1,0:T(8,128)S(1)} %copy.5.init_ref), custom_call_target="tpu_custom_call" | custom-call | tf_op jit(solution)/shard_map/pallas_call | solution.py:358
  178.6 0.8 copy.8
  179.4 1.0 copy.9
Async XLA Ops:
  1.4 1.6 copy-start
  3.0 0.7 copy-start.1
